TPU v7x, 32 devices: a whole 2x2x4 slice. The times are simulated.
32 devices in a mesh: seg: 16 (over z, y, x), dir: 2 (over core).
Axes of the slice: x: 2, y: 2, z: 4, core: 2. Of those that a mesh axis runs over, the one named last changes fastest.
Arguments:
- strain: float32 [128, 8, 6, 8192], P('seg'), may hold values from -6 to 6
- valid_flags: int32 [128, 8], P('seg'), may hold values from 0 to 1, as said below
- direction_ids: int32 [1024], P('dir'), may hold values from 0 to 3071
- grid_patterns: float32 [3072, 6], replicated, may hold values from -1 to 1
- grid_delays: float32 [3072, 3], replicated, may hold values from -40 to 40
Outputs:
- peak: float32 [8, 8192], P(None, 'seg')
- dir_score: float32 [8, 1024], P(None, 'dir')
Inputs may be any that keep to these rules, and one draw needn't show every extreme that they name: `valid_flags`: in every draw one window has no usable segment.
All inputs are finite; a program needn't handle non-finite values.
Results may differ from a plain program's by a relative error of at most 0.0001.
Values sent between devices are 32-bit elements; how exact they have to be, the bound alone decides.
No kernel may reach another device: no remote copies, remote signals or barrier semaphores. Data moves between devices by JAX's collectives and lax.ppermute only.
A program may use at most 64 MiB of HBM per device.

v0:
```python
import math
import jax
import jax.numpy as jnp
from jax import lax
from jax.sharding import PartitionSpec as P

F = 8192
PAIRS = ((0, 1), (0, 2), (1, 2))


def spectra(strain, valid_flags):
    weight = valid_flags.astype(jnp.float32)[:, :, None]
    real_part = strain[:, :, 0:3, :]
    imag_part = strain[:, :, 3:6, :]
    parts = []
    for d in range(3):
        parts.append(
            jnp.sum(
                weight
                * (
                    real_part[:, :, d] * real_part[:, :, d]
                    + imag_part[:, :, d] * imag_part[:, :, d]
                ),
                0,
            )
        )
    for d, e in PAIRS:
        parts.append(
            jnp.sum(
                weight
                * (
                    real_part[:, :, d] * real_part[:, :, e]
                    + imag_part[:, :, d] * imag_part[:, :, e]
                ),
                0,
            )
        )
    for d, e in PAIRS:
        parts.append(
            jnp.sum(
                weight
                * (
                    imag_part[:, :, d] * real_part[:, :, e]
                    - real_part[:, :, d] * imag_part[:, :, e]
                ),
                0,
            )
        )
    return jnp.stack(parts, 0)


def null_vectors(rows):
    plus = rows[:, 0:3]
    cross = rows[:, 3:6]
    first = plus[:, 1] * cross[:, 2] - plus[:, 2] * cross[:, 1]
    second = plus[:, 2] * cross[:, 0] - plus[:, 0] * cross[:, 2]
    third = plus[:, 0] * cross[:, 1] - plus[:, 1] * cross[:, 0]
    null = jnp.stack([first, second, third], 1)
    norm2 = jnp.maximum(jnp.sum(null * null, 1), 0.25)
    return (null, norm2)


def project(cov, first_bin, null, norm2, delays, count, total_bins):
    width = cov.shape[2]
    freq = (first_bin + jnp.arange(width, dtype=jnp.int32)).astype(jnp.float32) * (
        2.0 * math.pi / total_bins
    )
    energy = jnp.zeros((null.shape[0], cov.shape[1], width), jnp.float32)
    for d in range(3):
        energy = energy + (null[:, d] * null[:, d])[:, None, None] * cov[d][None]
    for index, (d, e) in enumerate(PAIRS):
        angle = (delays[:, d] - delays[:, e])[:, None] * freq[None, :]
        factor = (2.0 * null[:, d] * null[:, e])[:, None, None]
        energy = energy + factor * (
            jnp.cos(angle)[:, None, :] * cov[3 + index][None]
            + jnp.sin(angle)[:, None, :] * cov[6 + index][None]
        )
    return energy / (norm2[:, None, None] * jnp.maximum(count, 1.0)[None, :, None])


def shards(strain, valid_flags, direction_ids, grid_patterns, grid_delays):
    grid_points = grid_patterns.shape[0]
    one_hot = (direction_ids[:, None] == jnp.arange(grid_points, dtype=jnp.int32)[None, :]).astype(
        jnp.float32
    )
    table = jnp.concatenate([grid_patterns, grid_delays], 1)
    picked = jnp.dot(
        one_hot, table, precision=lax.Precision.HIGHEST, preferred_element_type=jnp.float32
    )
    null, norm2 = null_vectors(picked[:, 0:6])
    delays = picked[:, 6:9]
    count_part = jnp.sum(valid_flags.astype(jnp.float32), 0)
    bin_share = F // lax.axis_size("seg")
    first_bin = lax.axis_index("seg") * bin_share
    cov = lax.psum_scatter(spectra(strain, valid_flags), "seg", scatter_dimension=2, tiled=True)
    count = lax.psum(count_part, "seg")
    power = project(cov, first_bin, null, norm2, delays, count, F)
    peak_part = jnp.max(power, 0)
    score = lax.psum(jnp.sum(power, 2) / F, "seg")
    peak = lax.pmax(peak_part, "dir")
    return (peak, score.T)


def solution(mesh):
    placed = (P("seg", None, None, None), P("seg", None), P("dir"), P(), P())
    return jax.shard_map(
        shards,
        mesh=mesh,
        in_specs=placed,
        out_specs=(P(None, "seg"), P(None, "dir")),
        check_vma=False,
    )
```

profile of v0, /device:TPU:0, one launch (start us, length us, event | category | flops | bytes accessed | tf_op | source)
XLA Modules:
  0.0 199.6 jit_solution(11500045621607774981)
XLA Ops:
  7.2 0.0 reduce-scatter.2.cloned.1.call-start
  7.2 0.7 convert_element_type.12
  7.9 6.5 %fusion.34 = (f32[8,8192]{1,0:T(8,128)S(1)}, f32[8,8192]{1,0:T(8,128)S(1)}, f32[8,8192]{1,0:T(8,128)S(1)}, f32[8,8192]{1,0:T(8,128)S(1)}, f32[8,8192]{1,0:T(8,12...) fusion(f32[8,8,6,8192]{3,1,2,0:T(8,128)} %param.5, ...), kind=kLoop, calls=%fused_computation.48 | loop fusion | flops 23003136 | bytes 14942464 | tf_op jit(solution)/shard_map/reduce_sum | solution.py:40
  14.5 0.0 copy-start.1
  14.5 0.0 copy-start.2
  14.5 0.0 copy-start.3
  14.6 0.0 copy-start.4
  14.7 0.0 copy-start
  14.7 1.4 copy-done
  16.1 0.0 reduce-scatter.2.cloned.1.call-update
  16.1 0.0 copy-done.1
  16.2 43.8 %psum.14 = f32[8]{0:T(128)S(1)} all-reduce(f32[8]{0:T(128)S(1)} %convert_reduce_fusion), channel_id=1, replica_groups=mesh['seg'=16,'dir'=2] {'seg'}, use_global_device_ids=true, to_apply=%region_12.0 | all-reduce | flops 8 | bytes 64 | tf_op jit(solution)/shard_map/psum | solution.py:96
  60.0 0.0 copy-done.2
  60.0 0.0 copy-done.3
  60.0 0.0 copy-done.4
  60.0 3.0 %fusion = f32[512,9]{0,1:T(8,128)S(1)} fusion(s32[512]{0:T(512)S(1)} %copy-done.4, f32[3072,3]{0,1:T(4,128)S(1)} %copy-done.3, f32[3072,6]{0,1:T(8,128)S(1)} %copy-done.2), kind=kOutput, calls=%fused_computation.2 | convolution fusion | flops 171469824 | bytes 131072 | tf_op jit(solution)/shard_map/dot_general | solution.py:87
  63.0 0.1 slice_subtract_fusion.2
  63.1 0.1 broadcast_multiply_fusion
  63.2 12.5 %multiply_cosine_fusion.2 = (f32[512,512]{1,0:T(8,128)S(1)}, f32[512,512]{1,0:T(8,128)S(1)}, f32[512,512]{1,0:T(8,128)S(1)}, f32[512,512]{1,0:T(8,128)}, f32[512,512]{1,0:T(8,128)}, /*index=5*/f32[512,512]{1,0:T(8,128)}) fusion(f32[512]{0:T(512)S(1)} %convert_multiply_fusion, f32[512]{0:T(512)S(1)} %bitcast.242, f32[512]{0:T(512)S(1)} %bitcast.243, ...), kind=kLoop, calls=%fused_computation.63 | loop fusion | flops 786432 | bytes 6299648 | tf_op jit(solution)/shard_map/cos | solution.py:75
  75.7 25.3 %reduce-scatter.2.cloned.1.call-done = f32[9,8,512]{2,1,0:T(8,128)} async-done(((f32[9,8,8192]{2,1,0:T(8,128)}), f32[9,8,512]{2,1,0:T(8,128)}) %reduce-scatter.2.cloned.1.call-update) | async-done | bytes 147472 | tf_op jit(solution)/shard_map/reduce_scatter | solution.py:95
  101.0 0.9 slice_bitcast_fusion.8
  101.9 10.6 %fusion.44 = (f32[512,8]{1,0:T(8,128)S(1)}, f32[8,512]{1,0:T(8,128)S(1)}) fusion(f32[512,8]{1,0:T(8,128)S(1)} %broadcast_multiply_fusion, f32[8,512]{1,0:T(8,128)S(1)} %get-tuple-element.23, f32[512,512]{1,0:T(8,128)} %get-tuple-element.51, f32[8,512]{1,0:T(8,128)S(1)} %get-tuple-element.24, f32[512,512]{1,0:T(8,128)} %get-tuple-element.52, ...), kind=kLoop, calls=%fused_computation.102 | loop fusion | flops 48226304 | bytes 6500352 | tf_op jit(solution)/shard_map/reduce_sum | solution.py:99
  112.5 75.6 %psum.15 = f32[8,512]{0,1:T(8,128)S(1)} all-reduce(f32[8,512]{0,1:T(8,128)S(1)} %multiply_bitcast_fusion), channel_id=1, replica_groups=mesh['seg'=16,'dir'=2] {'seg'}, use_global_device_ids=true, to_apply=%region_16.0 | all-reduce | flops 4096 | bytes 32768 | tf_op jit(solution)/shard_map/psum | solution.py:99
  188.1 0.7 copy.31
  188.8 3.9 %pmax.7 = f32[8,512]{1,0:T(8,128)} all-reduce(f32[8,512]{1,0:T(8,128)S(1)} %get-tuple-element.14), channel_id=1, replica_groups=mesh['seg'=16,'dir'=2] {'dir'}, use_global_device_ids=true, to_apply=%region_14.0 | all-reduce | flops 4096 | bytes 32768 | tf_op jit(solution)/shard_map/pmax | solution.py:100
  (17 shorter events, 0.3 us)
Async XLA Ops:
  7.2 93.9 %reduce-scatter.2.cloned.1.call-start = ((), (), s32[]{:S(2)}) async-start(), calls=%async_computation.1 | async-start | bytes 2506752 | tf_op jit(solution)/shard_map/reduce_scatter | solution.py:95
  14.5 1.6 copy-start.1
  14.5 45.4 %copy-start.2 = (f32[3072,6]{0,1:T(8,128)S(1)}, f32[3072,6]{0,1:T(8,128)}, u32[]{:S(2)}) copy-start(f32[3072,6]{0,1:T(8,128)} %param.8) | copy-start | bytes 221188
  14.5 45.4 %copy-start.3 = (f32[3072,3]{0,1:T(4,128)S(1)}, f32[3072,3]{0,1:T(4,128)}, u32[]{:S(2)}) copy-start(f32[3072,3]{0,1:T(4,128)} %param.9) | copy-start | bytes 110596
  14.6 45.4 %copy-start.4 = (s32[512]{0:T(512)S(1)}, s32[512]{0:T(512)}, u32[]{:S(2)}) copy-start(s32[512]{0:T(512)} %param.7) | copy-start | bytes 6148
  14.7 1.4 copy-start
Sparse Core Ops, SparseCore 0:
  16.2 84.7 reduce-scatter.1
where the time goes:
time: 200 us
  blocking collectives  123 us (62%)
  other arithmetic  30.5 us (15%)
  waiting for transfers between devices  25.3 us (13%)
  between operations  14.2 us (7%)
  local copies, waits for them, and re-layouts  3.19 us (2%)
  matrix products  2.97 us (1%)
    psum x1, blocking collectives, shards(): score = lax.psum(jnp.sum(power, 2) / F, 'seg')  75.6 us
    psum x1, blocking collectives, shards(): count = lax.psum(count_part, 'seg')  43.8 us
    reduce_scatter x1, waiting for transfers between devices, shards(): lax.psum_scatter(spectra(strain, valid_flags), 'seg', scatter_dimension=2...  25.3 us
    cos x1, other arithmetic, project(): jnp.cos(angle)[:, None, :] * cov[3 + index][None]  12.5 us
    reduce_sum x1, other arithmetic, shards(): score = lax.psum(jnp.sum(power, 2) / F, 'seg')  10.6 us
    reduce_sum x1, other arithmetic, spectra(): jnp.sum(weight * (imag_part[:, :, d] * real_part[:, :, e] - real_part[:,...  6.48 us
  transfers between devices with their start and end apart: 1, of which 1 were waited for; matrix products, arithmetic and copies ran while one was open for 8% of the time, Pallas kernels for 0%

commit v1 on v0

--- a/solution.py
+++ b/solution.py
@@ -96,7 +96,7 @@
     count = lax.psum(count_part, "seg")
     power = project(cov, first_bin, null, norm2, delays, count, F)
     peak_part = jnp.max(power, 0)
-    score = lax.psum(jnp.sum(power, 2) / F, "seg")
+    score = jnp.sum(lax.all_gather(jnp.sum(power, 2) / F, "seg"), axis=0)
     peak = lax.pmax(peak_part, "dir")
     return (peak, score.T)
 

time: 200 us -> 164 us (0.82)
  blocking collectives: 123 us -> 86 us
    psum x1 -> x0, blocking collectives: 75.6 us -> none  [shards(): score = lax.psum(jnp.sum(power, 2) / F, 'seg')]
    all_gather x0 -> x1, blocking collectives: none -> 38.2 us  [shards(): score = jnp.sum(lax.all_gather(jnp.sum(power, 2) / F, 'seg'), axis=0)]
    reduce_sum x1 -> x2, other arithmetic: 10.6 us -> 11.9 us  [shards(): score = jnp.sum(lax.all_gather(jnp.sum(power, 2) / F, 'seg'), axis=0)]
  transfers between devices with their start and end apart: 1 -> 1, of which waited for: 1 -> 1; matrix products, arithmetic and copies ran while one was open for 8% -> 10% of each run, Pallas kernels for 0% -> 0%
where the time goes in v1:
time: 164 us
  blocking collectives  86 us (52%)
  other arithmetic  31.8 us (19%)
  waiting for transfers between devices  25.3 us (15%)
  between operations  14.2 us (9%)
  local copies, waits for them, and re-layouts  3.52 us (2%)
  matrix products  2.97 us (2%)
    psum x1, blocking collectives, shards(): count = lax.psum(count_part, 'seg')  43.8 us
    all_gather x1, blocking collectives, shards(): score = jnp.sum(lax.all_gather(jnp.sum(power, 2) / F, 'seg'), axis=0)  38.2 us
    reduce_scatter x1, waiting for transfers between devices, shards(): lax.psum_scatter(spectra(strain, valid_flags), 'seg', scatter_dimension=2...  25.3 us
    cos x1, other arithmetic, project(): jnp.cos(angle)[:, None, :] * cov[3 + index][None]  12.5 us
    reduce_sum x2, other arithmetic, shards(): score = jnp.sum(lax.all_gather(jnp.sum(power, 2) / F, 'seg'), axis=0)  11.9 us
    reduce_sum x1, other arithmetic, spectra(): jnp.sum(weight * (imag_part[:, :, d] * real_part[:, :, e] - real_part[:,...  6.48 us
    pmax x1, blocking collectives, shards(): peak = lax.pmax(peak_part, 'dir')  3.94 us
  transfers between devices with their start and end apart: 1, of which 1 were waited for; matrix products, arithmetic and copies ran while one was open for 10% of the time, Pallas kernels for 0%

profile of v1, /device:TPU:0, one launch (start us, length us, event | category | flops | bytes accessed | tf_op | source)
XLA Modules:
  0.0 163.9 jit_solution(3993309659040922456)
XLA Ops:
  7.2 0.0 reduce-scatter.2.cloned.1.call-start
  7.2 0.7 convert_element_type.12
  7.9 6.5 %fusion.34 = (f32[8,8192]{1,0:T(8,128)S(1)}, f32[8,8192]{1,0:T(8,128)S(1)}, f32[8,8192]{1,0:T(8,128)S(1)}, f32[8,8192]{1,0:T(8,128)S(1)}, f32[8,8192]{1,0:T(8,12...) fusion(f32[8,8,6,8192]{3,1,2,0:T(8,128)} %param.5, ...), kind=kLoop, calls=%fused_computation.48 | loop fusion | flops 23003136 | bytes 14942464 | tf_op jit(solution)/shard_map/reduce_sum | solution.py:40
  14.5 0.0 copy-start.1
  14.5 0.0 copy-start.2
  14.5 0.0 copy-start.3
  14.6 0.0 copy-start.4
  14.7 0.0 copy-start
  14.7 1.4 copy-done
  16.1 0.0 reduce-scatter.2.cloned.1.call-update
  16.1 0.0 copy-done.1
  16.2 43.8 %psum.7 = f32[8]{0:T(128)S(1)} all-reduce(f32[8]{0:T(128)S(1)} %convert_reduce_fusion), channel_id=1, replica_groups=mesh['seg'=16,'dir'=2] {'seg'}, use_global_device_ids=true, to_apply=%region_12.0 | all-reduce | flops 8 | bytes 64 | tf_op jit(solution)/shard_map/psum | solution.py:96
  60.0 0.0 copy-done.2
  60.0 0.0 copy-done.3
  60.0 0.0 copy-done.4
  60.0 3.0 %fusion = f32[512,9]{0,1:T(8,128)S(1)} fusion(s32[512]{0:T(512)S(1)} %copy-done.4, f32[3072,3]{0,1:T(4,128)S(1)} %copy-done.3, f32[3072,6]{0,1:T(8,128)S(1)} %copy-done.2), kind=kOutput, calls=%fused_computation.2 | convolution fusion | flops 171469824 | bytes 131072 | tf_op jit(solution)/shard_map/dot_general | solution.py:87
  63.0 0.1 slice_subtract_fusion.2
  63.1 0.1 broadcast_multiply_fusion
  63.2 12.5 %multiply_cosine_fusion.2 = (f32[512,512]{1,0:T(8,128)S(1)}, f32[512,512]{1,0:T(8,128)S(1)}, f32[512,512]{1,0:T(8,128)S(1)}, f32[512,512]{1,0:T(8,128)}, f32[512,512]{1,0:T(8,128)}, /*index=5*/f32[512,512]{1,0:T(8,128)}) fusion(f32[512]{0:T(512)S(1)} %convert_multiply_fusion, f32[512]{0:T(512)S(1)} %bitcast.244, f32[512]{0:T(512)S(1)} %bitcast.245, ...), kind=kLoop, calls=%fused_computation.63 | loop fusion | flops 786432 | bytes 6299648 | tf_op jit(solution)/shard_map/cos | solution.py:75
  75.7 25.3 %reduce-scatter.2.cloned.1.call-done = f32[9,8,512]{2,1,0:T(8,128)} async-done(((f32[9,8,8192]{2,1,0:T(8,128)}), f32[9,8,512]{2,1,0:T(8,128)}) %reduce-scatter.2.cloned.1.call-update) | async-done | bytes 147472 | tf_op jit(solution)/shard_map/reduce_scatter | solution.py:95
  101.0 0.9 slice_bitcast_fusion.8
  101.9 11.3 %fusion.44 = (f32[512,8]{1,0:T(8,128)}, f32[8,512]{1,0:T(8,128)S(1)}) fusion(f32[512,8]{1,0:T(8,128)S(1)} %broadcast_multiply_fusion, f32[8,512]{1,0:T(8,128)S(1)} %get-tuple-element.21, f32[512,512]{1,0:T(8,128)} %get-tuple-element.49, f32[8,512]{1,0:T(8,128)S(1)} %get-tuple-element.22, f32[512,512]{1,0:T(8,128)} %get-tuple-element.50, ...), kind=kLoop, calls=%fused_computation.102 | loop fusion | flops 48226304 | bytes 6500352 | tf_op jit(solution)/shard_map/reduce_sum | solution.py:99
  113.2 1.0 copy.44
  114.2 38.2 %all-gather = f32[8192,8]{0,1:T(8,128)S(1)} all-gather(f32[512,8]{0,1:T(8,128)S(1)} %broadcast_multiply_fusion.1), channel_id=2, replica_groups=mesh['seg'=16,'dir'=2] {'seg'}, dimensions={0}, use_global_device_ids=true | all-gather | bytes 278528 | tf_op jit(solution)/shard_map/all_gather | solution.py:99
  152.5 3.9 %pmax.7 = f32[8,512]{1,0:T(8,128)} all-reduce(f32[8,512]{1,0:T(8,128)S(1)} %get-tuple-element.12), channel_id=1, replica_groups=mesh['seg'=16,'dir'=2] {'dir'}, use_global_device_ids=true, to_apply=%region_14.0 | all-reduce | flops 4096 | bytes 32768 | tf_op jit(solution)/shard_map/pmax | solution.py:100
  156.4 0.6 reduce_sum.129
  (17 shorter events, 0.3 us)
Async XLA Ops:
  7.2 93.9 %reduce-scatter.2.cloned.1.call-start = ((), (), s32[]{:S(2)}) async-start(), calls=%async_computation.1 | async-start | bytes 2506752 | tf_op jit(solution)/shard_map/reduce_scatter | solution.py:95
  14.5 1.6 copy-start.1
  14.5 45.4 %copy-start.2 = (f32[3072,6]{0,1:T(8,128)S(1)}, f32[3072,6]{0,1:T(8,128)}, u32[]{:S(2)}) copy-start(f32[3072,6]{0,1:T(8,128)} %param.8) | copy-start | bytes 221188
  14.5 45.4 %copy-start.3 = (f32[3072,3]{0,1:T(4,128)S(1)}, f32[3072,3]{0,1:T(4,128)}, u32[]{:S(2)}) copy-start(f32[3072,3]{0,1:T(4,128)} %param.9) | copy-start | bytes 110596
  14.6 45.4 %copy-start.4 = (s32[512]{0:T(512)S(1)}, s32[512]{0:T(512)}, u32[]{:S(2)}) copy-start(s32[512]{0:T(512)} %param.7) | copy-start | bytes 6148
  14.7 1.4 copy-start
Sparse Core Ops, SparseCore 0:
  16.2 84.7 reduce-scatter.1
